TPU v7x, 256 devices: a whole 4x4x8 slice. The times are simulated.
256 devices in a mesh: head: 16 (over z, core), tail: 16 (over y, x).
Axes of the slice: x: 4, y: 4, z: 8, core: 2. Of those that a mesh axis runs over, the one named last changes fastest.
Arguments:
- head_emb: bfloat16 [131072, 800], P(('head', 'tail')), may hold values from -48 to 48
- head_state: float32 [131072], P(('head', 'tail')), may hold values from 0.01 to 1
- tail_emb: bfloat16 [64, 128, 800], P('tail'), may hold values from -1.5 to 1.5
- tail_state: float32 [64, 128], P('tail'), may hold values from 0.01 to 1
- relation_emb: bfloat16 [1024, 800], replicated, may hold values from -3.5 to 3.5
- head_rows: int32 [1024, 256], P(('head', 'tail')), may hold values from 0 to 511
- relations: int32 [1024, 256], P(('head', 'tail')), may hold values from 0 to 1023
- tail_offsets: int32 [1024, 256], P(('head', 'tail')), may hold values from 0 to 127
- tail_owner: int32 [1024, 1], P(('head', 'tail')), may hold values from 0 to 15; in each aligned block of 4 rows (0 to 3, 4 to 7, ...) at most 2 rows name the same one
- tail_local: int32 [1024], P(('head', 'tail')), may hold values from 0 to 3
- block_count: int32 [256], P(('head', 'tail')), may hold values from 1 to 4, as said below
- neg_blocks: int32 [8], replicated, may hold values from 0 to 63, as said below
Outputs:
- head_new: bfloat16 [131072, 800], P(('head', 'tail'))
- head_state_new: float32 [131072], P(('head', 'tail'))
- tail_new: bfloat16 [64, 128, 800], P('tail')
- tail_state_new: float32 [64, 128], P('tail')
Inputs may be any that keep to these rules, and one draw needn't show every extreme that they name: `tail_owner`: no tail index owns the tail blocks of more than 2 edge block slots of one device, and in some devices one owns exactly 2. `block_count`: some device has all 4 slots live. `neg_blocks`: distinct tail blocks; the last tail block is always among them.
All inputs are finite; a program needn't handle non-finite values.
Results may differ from a plain program's by a relative error of at most 0.0012.
The roundings to bfloat16 on the way count: a program that leaves them out, or rounds other values in their place, can miss the bound.
Values may be sent and summed in bfloat16 or wider, within the bound.
A program may use at most 128 MiB of HBM per device.

v0:
```python
import math
import jax
import jax.numpy as jnp
from jax import lax
from jax.sharding import PartitionSpec as P

LEARN_RATE = 0.3


def complex_product(left, right):
    half_width = left.shape[-1] // 2
    left_re, left_im = (left[..., :half_width], left[..., half_width:])
    right_re, right_im = (right[..., :half_width], right[..., half_width:])
    return jnp.concatenate(
        [left_re * right_re - left_im * right_im, left_re * right_im + left_im * right_re], axis=-1
    )


def conj_product(left, right):
    half_width = left.shape[-1] // 2
    left_re, left_im = (left[..., :half_width], left[..., half_width:])
    right_re, right_im = (right[..., :half_width], right[..., half_width:])
    return jnp.concatenate(
        [left_re * right_re + left_im * right_im, left_im * right_re - left_re * right_im], axis=-1
    )


def row_adagrad(embedding, adagrad_state, gradient):
    state_next = adagrad_state + jnp.mean(gradient * gradient, axis=-1)
    updated = (
        embedding.astype(jnp.float32) - LEARN_RATE * gradient / jnp.sqrt(state_next)[..., None]
    )
    return (updated.astype(jnp.bfloat16), state_next)


def head_sum(tail_grad):
    return lax.psum(tail_grad, "head")


def per_device(
    head_emb,
    head_state,
    tail_emb,
    tail_state,
    relation_emb,
    head_rows,
    relations,
    tail_offsets,
    tail_owner,
    tail_local,
    block_count,
    neg_blocks,
):
    block_total = tail_local.shape[0]
    edge_count = head_rows.shape[1]
    row_width = head_emb.shape[1]
    span_rows = tail_emb.shape[1]
    owned_blocks = tail_emb.shape[0]
    peer_count = lax.axis_size("tail")
    tail_rank = lax.axis_index("tail")
    capacity = max(2, (2 * block_total + peer_count - 1) // peer_count)
    owner_rank = tail_owner[:, 0]
    positions = jnp.arange(block_total, dtype=jnp.int32)
    same_owner = owner_rank[:, None] == owner_rank[None, :]
    earlier = positions[None, :] < positions[:, None]
    slot_index = jnp.sum((same_owner & earlier).astype(jnp.int32), axis=1)
    slot_place = owner_rank * capacity + slot_index
    global_block = owner_rank * owned_blocks + tail_local
    partition = lax.all_gather(tail_emb, "tail", axis=0, tiled=True)
    chosen = jnp.take(partition, global_block, axis=0)
    mine_ids = neg_blocks - tail_rank * owned_blocks
    is_mine = (mine_ids >= 0) & (mine_ids < owned_blocks)
    own_negs = jnp.where(
        is_mine[:, None, None],
        jnp.take(tail_emb, jnp.clip(mine_ids, 0, owned_blocks - 1), axis=0),
        jnp.zeros((), jnp.bfloat16),
    )
    negatives = lax.psum(own_negs.astype(jnp.float32).astype(jnp.bfloat16), "tail").reshape(
        -1, row_width
    )
    total_edges = block_total * edge_count
    flat_rows = head_rows.reshape(-1)
    block_of = jnp.arange(total_edges, dtype=jnp.int32) // edge_count
    live_mask = (block_of < block_count[0]).astype(jnp.float32)
    tail_index = block_of * span_rows + tail_offsets.reshape(-1)
    tail_vectors = jnp.take(chosen.reshape(-1, row_width), tail_index, axis=0)
    relation_vectors = jnp.take(relation_emb, relations.reshape(-1), axis=0)
    head_vectors = jnp.take(head_emb, flat_rows, axis=0)
    query = complex_product(
        head_vectors.astype(jnp.float32), relation_vectors.astype(jnp.float32)
    ).astype(jnp.bfloat16)
    per_group = math.gcd(block_total, max(1, 512 // edge_count))
    group_rows = per_group * edge_count
    group_count = total_edges // group_rows

    def grouped(values):
        return values.reshape((group_count, group_rows) + values.shape[1:])

    def score_group(neg_total, group_items):
        query_rows, tail_rows, live_rows = group_items
        query_float = query_rows.astype(jnp.float32)
        positive = jnp.sum(query_float * tail_rows.astype(jnp.float32), axis=1)
        negative = lax.dot_general(
            query_rows, negatives, (((1,), (1,)), ((), ())), preferred_element_type=jnp.float32
        )
        largest = jnp.maximum(positive, jnp.max(negative, axis=1))
        pos_exp = jnp.exp(positive - largest)
        neg_exp = jnp.exp(negative - largest[:, None])
        denominator = pos_exp + jnp.sum(neg_exp, axis=1)
        pos_grad = (pos_exp / denominator - 1.0) * live_rows
        neg_grad = (neg_exp / denominator[:, None] * live_rows[:, None]).astype(jnp.bfloat16)
        query_grad = pos_grad[:, None] * tail_rows.astype(jnp.float32) + jnp.dot(
            neg_grad, negatives, preferred_element_type=jnp.float32
        )
        tail_part = pos_grad[:, None] * query_float
        neg_total = neg_total + lax.dot_general(
            neg_grad, query_rows, (((0,), (0,)), ((), ())), preferred_element_type=jnp.float32
        )
        return (neg_total, (query_grad, tail_part))

    neg_start = jnp.zeros((negatives.shape[0], row_width), jnp.float32)
    neg_part, (query_grad, tail_part) = lax.scan(
        score_group, neg_start, (grouped(query), grouped(tail_vectors), grouped(live_mask))
    )
    query_grad = query_grad.reshape(total_edges, row_width)
    tail_part = tail_part.reshape(total_edges, row_width)
    head_grad = (
        jnp.zeros(head_emb.shape, jnp.float32)
        .at[flat_rows]
        .add(conj_product(query_grad, relation_vectors.astype(jnp.float32)))
    )
    block_grad = (
        jnp.zeros((block_total * span_rows, row_width), jnp.float32)
        .at[tail_index]
        .add(tail_part)
        .astype(jnp.bfloat16)
    )
    outgoing = (
        jnp.zeros((peer_count * capacity, span_rows, row_width), jnp.bfloat16)
        .at[slot_place]
        .set(block_grad.reshape(block_total, span_rows, row_width))
    )
    outgoing = outgoing.reshape(peer_count, capacity, span_rows, row_width)
    slot_ids = (
        jnp.zeros((peer_count * capacity,), jnp.int32)
        .at[slot_place]
        .set(tail_local)
        .reshape(peer_count, capacity)
    )
    incoming, incoming_ids = (
        lax.all_to_all(outgoing, "tail", split_axis=0, concat_axis=0, tiled=True),
        lax.all_to_all(slot_ids, "tail", split_axis=0, concat_axis=0, tiled=True),
    )
    which_block = (
        incoming_ids.reshape(-1)[:, None] == jnp.arange(owned_blocks, dtype=jnp.int32)[None, :]
    ).astype(jnp.bfloat16)
    tail_grad = lax.dot_general(
        which_block,
        incoming.reshape(peer_count * capacity, span_rows * row_width),
        (((0,), (0,)), ((), ())),
        preferred_element_type=jnp.float32,
    )
    neg_weights = (
        (mine_ids[:, None] == jnp.arange(owned_blocks, dtype=jnp.int32)[None, :]) & is_mine[:, None]
    ).astype(jnp.float32)
    neg_all = lax.psum(neg_part, ("head", "tail"))
    tail_total = head_sum(tail_grad) + lax.dot_general(
        neg_weights,
        neg_all.reshape(neg_weights.shape[0], span_rows * row_width),
        (((0,), (0,)), ((), ())),
        precision=lax.Precision.HIGHEST,
        preferred_element_type=jnp.float32,
    )
    head_updated, head_state_updated = row_adagrad(head_emb, head_state, head_grad)
    tail_updated, tail_state_updated = row_adagrad(
        tail_emb, tail_state, tail_total.reshape(owned_blocks, span_rows, row_width)
    )
    return (head_updated, head_state_updated, tail_updated, tail_state_updated)


def solution(mesh):
    placed = (
        P(("head", "tail"), None),
        P(("head", "tail")),
        P("tail", None, None),
        P("tail", None),
        P(),
        P(("head", "tail"), None),
        P(("head", "tail"), None),
        P(("head", "tail"), None),
        P(("head", "tail"), None),
        P(("head", "tail")),
        P(("head", "tail")),
        P(),
    )
    return jax.shard_map(
        per_device,
        mesh=mesh,
        in_specs=placed,
        out_specs=(
            P(("head", "tail"), None),
            P(("head", "tail")),
            P("tail", None, None),
            P("tail", None),
        ),
        check_vma=False,
    )
```

profile of v0, /device:TPU:1, one launch (start us, length us, event | category | flops | bytes accessed | tf_op | source)
XLA Modules:
  0.0 729.9 jit_solution(752198037437776522)
XLA Ops:
  7.2 0.7 all-gather.2.cloned.1.call-update
  7.9 0.9 convert_reduce_fusion
  9.5 0.7 scatter_custom_fusion.1
  10.2 0.7 all_to_all.9
  10.9 7.6 %all-to-all-start = ((s32[16,1,2]{2,1,0:T(1,128)}), s32[16,1,2]{2,1,0:T(1,128)S(1)}, u32[]{:S(2)}, u32[]{:S(2)}) async-start(s32[16,1,2]{2,1,0:T(1,128)} %bitcast.13), calls=%async_computation | async-start | bytes 16384 | tf_op jit(solution)/shard_map/all_to_all | solution.py:152
  19.2 0.9 gather_fusion.1
  20.1 1.4 select_select_fusion
  21.5 3.8 copy.82
  26.1 3.1 copy.79
  29.3 5.3 gather_fusion.3
  34.5 5.3 gather_fusion
  39.8 2.5 select_convert_fusion
  42.4 1.5 subtract_convert_fusion
  44.2 1.2 copy.80
  45.4 1.2 copy.81
  47.3 1.3 pad_maximum_fusion
  48.7 62.8 %all-gather.2.cloned.1.call-done = bf16[64,128,800]{1,2,0:T(8,128)(2,1)} async-done(((bf16[4,128,800]{1,2,0:T(8,128)(2,1)}), bf16[64,128,800]{1,2,0:T(8,128)(2,1)}) %all-gather.2.cloned.1.call-update) | async-done | bytes 13107216 | tf_op jit(solution)/shard_map/all_gather | solution.py:69
  111.5 5.4 gather_fusion.2
  117.0 1.3 copy.83
  118.2 1.4 bitcast_select_fusion
  119.6 5.3 gather_fusion.4
  124.9 3.3 broadcast_select_fusion
  128.2 3.5 copy.84
  131.6 81.5 %all-reduce.4.cloned.1.call-done = bf16[1024,800]{1,0:T(8,128)(2,1)} async-done(((bf16[1024,800]{1,0:T(8,128)(2,1)}), bf16[1024,800]{1,0:T(8,128)(2,1)}) %all-reduce.4.cloned.1.call-update) | async-done | bytes 1638416 | tf_op jit(solution)/shard_map/psum | solution.py:78
  213.2 30.7 %while.17 = (s32[]{:T(128)}, f32[1024,800]{0,1:T(8,128)}, f32[2,512,800]{1,2,0:T(8,128)}, f32[2,512,800]{1,2,0:T(8,128)}, bf16[2,512,800]{1,2,0:T(8,128)(2,1)S(1...) while((s32[]{:T(128)}, f32[1024,800]{0,1:T(8,128)}, ...), condition=%wide.region_5.7_spmd.clone, body=%wide.region_1.6_spmd.clone.sunk | while | flops 2527675904 | bytes 74365712 | solution.py:122
  213.2 3.0 fusion.55
  217.1 1.8 copy-done.7
  218.9 1.4 fusion.58
  220.3 1.8 copy-done.8
  222.1 1.5 multiply_dynamic-update-slice_fusion.2
  223.6 4.5 select_add_fusion.2
  228.1 3.0 fusion.55
  232.0 1.8 copy-done.7
  233.8 1.4 fusion.58
  235.3 1.8 copy-done.8
  237.0 1.4 multiply_dynamic-update-slice_fusion.2
  238.4 5.4 select_add_fusion.2
  243.9 4.4 copy.95
  248.2 10.8 %scatter_custom_fusion.2 = f32[512,800]{1,0:T(8,128)S(1)} fusion(s32[1024]{0:T(1024)S(1)} %bitcast.112, f32[1024,800]{1,0:T(8,128)} %bitcast.92, f32[]{:T(128)} %constant.133.clone.1), kind=kCustom, calls=%fused_computation.49 | custom fusion | flops 819200 | bytes 1638912 | tf_op jit(solution)/shard_map/scatter-add | solution.py:135
  259.1 1.1 convert_element_type.70
  260.2 1.5 copy.90
  261.7 3.6 broadcast_in_dim.108
  265.3 2.8 scatter_fusion
  268.1 4.6 all-to-all-start.1
  272.8 4.9 copy.92
  277.7 6.1 reshape.276
  283.8 1.1 copy-done.4
  284.9 1.3 copy.86
  287.4 4.4 copy.85
  291.8 75.6 %all-to-all-done.1 = bf16[16,2,128,800]{2,3,1,0:T(8,128)(2,1)} async-done(((bf16[16,2,128,800]{2,3,1,0:T(8,128)(2,1)}), bf16[16,2,128,800]{2,3,1,0:T(8,128)(2,1)}, u32[]{:S(2)}, u32[]{:S(2)}) %all-to-all-start.1) | async-done | bytes 6553632 | tf_op jit(solution)/shard_map/all_to_all | solution.py:151
  367.4 11.0 %copy.91 = bf16[16,2,128,800]{3,2,1,0:T(8,128)(2,1)} copy(bf16[16,2,128,800]{2,3,1,0:T(8,128)(2,1)} %all-to-all-done.1) | data formatting | bytes 13107200 | tf_op jit(solution)/shard_map/all_to_all | solution.py:151
  378.5 13.6 %reshape.275 = bf16[32,102400]{1,0:T(8,128)(2,1)} reshape(bf16[16,2,128,800]{3,2,1,0:T(8,128)(2,1)} %copy.91) | data formatting | bytes 13107200 | tf_op jit(solution)/shard_map/reshape | solution.py:159
  392.1 5.1 fusion.20
  397.3 6.6 multiply_add_fusion
  403.9 10.9 %scatter_custom_fusion = f32[512,800]{1,0:T(8,128)S(1)} fusion(s32[1024]{0:T(1024)S(1)} %bitcast.113, f32[1024,400]{1,0:T(8,128)} %get-tuple-element.225, f32[]{:T(128)} %constant.164, f32[1024,400]{1,0:T(8,128)} %get-tuple-element.224, f32[]{:T(128)} %constant.133.clone.1), kind=kCustom, calls=%fused_computation.32 | custom fusion | flops 1638400 | bytes 4915208 | tf_op jit(solution)/shard_map/scatter-add | solution.py:130
  415.5 1.4 subtract_convert_fusion.2
  417.0 2.1 copy.93
  419.1 172.2 %all-reduce.8.cloned.1.call-done = f32[8,102400]{1,0:T(8,128)} async-done(((f32[8,102400]{1,0:T(8,128)}), f32[8,102400]{1,0:T(8,128)}) %all-reduce.8.cloned.1.call-update) | async-done | bytes 3276816 | tf_op jit(solution)/shard_map/psum | solution.py:166
  591.3 116.5 %all-reduce.6.cloned.1.call-done = f32[4,102400]{1,0:T(4,128)} async-done(((f32[4,102400]{1,0:T(4,128)}), f32[4,102400]{1,0:T(4,128)}) %all-reduce.6.cloned.1.call-update) | async-done | bytes 1638416 | tf_op jit(solution)/shard_map/psum | solution.py:37
  707.9 5.1 broadcast_multiply_fusion
  713.0 3.0 mul.159
  716.2 3.1 mul.157
  719.8 1.3 subtract_convert_fusion.1
  721.1 2.2 copy.94
  (93 shorter events, 7.2 us)
Async XLA Ops:
  7.2 12.1 %copy-start.3 = (bf16[4,128,800]{1,2,0:T(8,128)(2,1)S(1)}, bf16[4,128,800]{1,2,0:T(8,128)(2,1)}, u32[]{:S(2)}) copy-start(bf16[4,128,800]{1,2,0:T(8,128)(2,1)} %param.18) | copy-start | bytes 2457604
  7.2 104.3 %all-gather.2.cloned.1.call-start = ((), (), s32[]{:S(2)}) async-start(), calls=%async_computation.3 | async-start | bytes 13926400 | tf_op jit(solution)/shard_map/all_gather | solution.py:69
  10.9 257.2 %all-to-all-start = ((s32[16,1,2]{2,1,0:T(1,128)}), s32[16,1,2]{2,1,0:T(1,128)S(1)}, u32[]{:S(2)}, u32[]{:S(2)}) async-start(s32[16,1,2]{2,1,0:T(1,128)} %bitcast.13), calls=%async_computation | async-start | bytes 16384 | tf_op jit(solution)/shard_map/all_to_all | solution.py:152
  18.5 194.7 %all-reduce.4.cloned.1.call-start = ((), (), s32[]{:S(2)}) async-start(), calls=%async_computation.2 | async-start | bytes 3670016 | tf_op jit(solution)/shard_map/psum | solution.py:78
  21.5 3.8 copy-start.12
  21.5 3.9 copy-start.15
  21.5 3.9 copy-start.16
  21.5 3.9 copy-start.9
  26.1 3.1 copy-start.10
  42.4 1.8 copy-start.1
  44.2 3.1 copy-start.11
  45.4 1.9 copy-start.6
  213.2 3.1 copy-start.2
  213.2 3.9 copy-start.17
  216.2 4.1 copy-start
  216.2 2.7 copy-start.7
  220.3 1.8 copy-start.8
  228.1 3.1 copy-start.2
  228.1 3.9 copy-start.17
  231.1 4.1 copy-start
  231.1 2.7 copy-start.7
  235.2 1.8 copy-start.8
  268.1 99.3 %all-to-all-start.1 = ((bf16[16,2,128,800]{2,3,1,0:T(8,128)(2,1)}), bf16[16,2,128,800]{2,3,1,0:T(8,128)(2,1)}, u32[]{:S(2)}, u32[]{:S(2)}) async-start(bf16[16,2,128,800]{2,3,1,0:T(8,128)(2,1)} %bitcast.86), calls=%async_computation.1 | async-start | bytes 13107200 | tf_op jit(solution)/shard_map/all_to_all | solution.py:151
  272.7 318.6 %all-reduce.8.cloned.1.call-start = ((), (), s32[]{:S(2)}) async-start(), calls=%async_computation.5 | async-start | bytes 6553600 | tf_op jit(solution)/shard_map/psum | solution.py:166
  283.7 1.1 copy-start.4
  283.7 424.1 %all-reduce.6.cloned.1.call-start = ((), (), s32[]{:S(2)}) async-start(), calls=%async_computation.4 | async-start | bytes 3276800 | tf_op jit(solution)/shard_map/psum | solution.py:37
  403.9 11.1 %copy-start.13 = (f32[512]{0:T(512)S(1)}, f32[512]{0:T(512)}, u32[]{:S(2)}) copy-start(f32[512]{0:T(512)} %param.17) | copy-start | bytes 6148
  716.1 3.1 copy-start.14
  716.2 3.7 copy-start.5
Sparse Core Ops, SparseCore 0:
  10.4 101.0 all-gather.1
  114.9 98.2 all-reduce.3
  283.9 307.4 all-reduce.7
  593.6 114.2 all-reduce.5
where the time goes:
time: 731 us; the launch traced here: 730 us
  waiting for transfers between devices  509 us (70%)
  local copies, waits for them, and re-layouts  111 us (15%)
  other arithmetic  52.5 us (7%)
  matrix products  29.1 us (4%)
  between operations  14.8 us (2%)
  starting transfers between devices  12.4 us (2%)
    psum x1, waiting for transfers between devices, per_device(): neg_all = lax.psum(neg_part, ('head', 'tail'))  172 us
    psum x1, waiting for transfers between devices, head_sum(): return lax.psum(tail_grad, 'head')  117 us
    psum x1, waiting for transfers between devices, per_device(): lax.psum(own_negs.astype(jnp.float32).astype(jnp.bfloat16), 'tail')  81.5 us
    all_to_all x1, waiting for transfers between devices, per_device(): lax.all_to_all(outgoing, 'tail', split_axis=0, concat_axis=0, tiled=True)  75.6 us
    all_gather x1, waiting for transfers between devices, per_device(): partition = lax.all_gather(tail_emb, 'tail', axis=0, tiled=True)  62.8 us
  transfers between devices with their start and end apart: 6, of which 5 were waited for; matrix products, arithmetic and copies ran while one was open for 23% of the time, Pallas kernels for 0%

commit v1 on v0

--- a/solution.py
+++ b/solution.py
@@ -66,7 +66,9 @@
     slot_index = jnp.sum((same_owner & earlier).astype(jnp.int32), axis=1)
     slot_place = owner_rank * capacity + slot_index
     global_block = owner_rank * owned_blocks + tail_local
-    partition = lax.all_gather(tail_emb, "tail", axis=0, tiled=True)
+    partition = jnp.concatenate(
+        lax.all_to_all(jnp.stack([tail_emb] * lax.axis_size("tail")), "tail", 0, 0), axis=0
+    )
     chosen = jnp.take(partition, global_block, axis=0)
     mine_ids = neg_blocks - tail_rank * owned_blocks
     is_mine = (mine_ids >= 0) & (mine_ids < owned_blocks)

time: 731 us -> 801 us (1.096)
  waiting for transfers between devices: 509 us -> 563 us
  local copies, waits for them, and re-layouts: 111 us -> 120 us
    all_to_all x0 -> x1, waiting for transfers between devices: none -> 173 us  [per_device(): lax.all_to_all(jnp.stack([tail_emb] * lax.axis_size('tail')), 'tail', 0, 0)]
    all_gather x1 -> x0, waiting for transfers between devices: 62.8 us -> none  [per_device(): partition = lax.all_gather(tail_emb, 'tail', axis=0, tiled=True)]
    psum x1, waiting for transfers between devices: 81.5 us -> 26.4 us  [per_device(): lax.psum(own_negs.astype(jnp.float32).astype(jnp.bfloat16), 'tail')]
    another operation x0 -> x1, local copies, waits for them, and re-layouts: none -> 8.4 us  [per_device(): jnp.stack([tail_emb] * lax.axis_size('tail'))]
  transfers between devices with their start and end apart: 6 -> 6, of which waited for: 5 -> 5; matrix products, arithmetic and copies ran while one was open for 23% -> 21% of each run, Pallas kernels for 0% -> 0%
where the time goes in v1:
time: 801 us; the launch traced here: 794 us
  waiting for transfers between devices  563 us (70%)
  local copies, waits for them, and re-layouts  120 us (15%)
  other arithmetic  50.1 us (6%)
  matrix products  29 us (4%)
  starting transfers between devices  16.6 us (2%)
  between operations  15 us (2%)
    all_to_all x1, waiting for transfers between devices, per_device(): lax.all_to_all(jnp.stack([tail_emb] * lax.axis_size('tail')), 'tail', 0, 0)  173 us
    psum x1, waiting for transfers between devices, per_device(): neg_all = lax.psum(neg_part, ('head', 'tail'))  172 us
    psum x1, waiting for transfers between devices, head_sum(): return lax.psum(tail_grad, 'head')  117 us
    all_to_all x1, waiting for transfers between devices, per_device(): lax.all_to_all(outgoing, 'tail', split_axis=0, concat_axis=0, tiled=True)  75.5 us
    psum x1, waiting for transfers between devices, per_device(): lax.psum(own_negs.astype(jnp.float32).astype(jnp.bfloat16), 'tail')  26.4 us
  transfers between devices with their start and end apart: 6, of which 5 were waited for; matrix products, arithmetic and copies ran while one was open for 21% of the time, Pallas kernels for 0%

profile of v1, /device:TPU:1, one launch (start us, length us, event | category | flops | bytes accessed | tf_op | source)
XLA Modules:
  0.0 793.6 jit_solution(10043907354034907498)
XLA Ops:
  7.2 8.4 %stack.2 = bf16[16,4,128,800]{2,3,1,0:T(8,128)(2,1)} broadcast(bf16[4,128,800]{1,2,0:T(8,128)(2,1)} %param.18), dimensions={1,2,3} | broadcast | bytes 13926400 | tf_op jit(solution)/shard_map/stack | solution.py:70
  15.6 7.7 all-to-all-start
  23.4 0.9 gather_fusion.1
  24.3 1.4 select_select_fusion
  25.7 3.8 copy.117
  30.2 3.0 copy.114
  33.3 5.3 gather_fusion.3
  38.6 5.3 gather_fusion
  43.9 2.5 select_convert_fusion
  46.5 1.5 subtract_convert_fusion
  48.3 1.2 copy.115
  49.5 1.2 copy.116
  52.2 0.7 all_to_all.13
  52.9 1.3 pad_maximum_fusion
  54.3 172.6 %all-to-all-done = bf16[16,4,128,800]{2,3,1,0:T(8,128)(2,1)} async-done(((bf16[16,4,128,800]{2,3,1,0:T(8,128)(2,1)}), bf16[16,4,128,800]{2,3,1,0:T(8,128)(2,1)}, u32[]{:S(2)}, u32[]{:S(2)}) %all-to-all-start) | async-done | bytes 13107232 | tf_op jit(solution)/shard_map/all_to_all | solution.py:70
  226.9 3.9 all-to-all-start.1
  230.8 5.4 gather_fusion.2
  236.3 1.3 copy.131
  237.6 1.4 bitcast_select_fusion
  238.9 5.3 gather_fusion.4
  244.2 3.1 broadcast_select_fusion
  247.3 3.5 copy.120
  250.8 26.4 %all-reduce.4.cloned.1.call-done = bf16[1024,800]{1,0:T(8,128)(2,1)} async-done(((bf16[1024,800]{1,0:T(8,128)(2,1)}), bf16[1024,800]{1,0:T(8,128)(2,1)}) %all-reduce.4.cloned.1.call-update) | async-done | bytes 1638416 | tf_op jit(solution)/shard_map/psum | solution.py:80
  277.1 30.4 %while.17 = (s32[]{:T(128)}, f32[1024,800]{0,1:T(8,128)}, f32[2,512,800]{1,2,0:T(8,128)}, f32[2,512,800]{1,2,0:T(8,128)}, bf16[2,512,800]{1,2,0:T(8,128)(2,1)S(1...) while((s32[]{:T(128)}, f32[1024,800]{0,1:T(8,128)}, ...), condition=%wide.region_5.7_spmd.clone, body=%wide.region_1.6_spmd.clone.sunk | while | flops 2527675904 | bytes 74365712 | solution.py:124
  277.1 3.0 fusion.55
  281.0 1.8 copy-done.7
  282.9 1.4 fusion.58
  284.3 1.7 copy-done.8
  286.0 1.5 multiply_dynamic-update-slice_fusion.2
  287.5 4.4 select_add_fusion.2
  291.9 3.0 fusion.55
  295.8 1.8 copy-done.7
  297.6 1.4 fusion.58
  299.1 1.7 copy-done.8
  300.8 1.4 multiply_dynamic-update-slice_fusion.2
  302.2 5.4 select_add_fusion.2
  307.6 4.4 copy.132
  311.9 10.7 %scatter_custom_fusion.2 = f32[512,800]{1,0:T(8,128)S(1)} fusion(s32[1024]{0:T(1024)S(1)} %bitcast.113, f32[1024,800]{1,0:T(8,128)} %bitcast.93, f32[]{:T(128)} %constant.133.clone.1), kind=kCustom, calls=%fused_computation.49 | custom fusion | flops 819200 | bytes 1638912 | tf_op jit(solution)/shard_map/scatter-add | solution.py:137
  322.6 1.0 convert_element_type.70
  323.7 1.5 copy.126
  325.2 3.6 broadcast_in_dim.108
  328.8 2.8 scatter_fusion
  331.6 4.6 all-to-all-start.2
  336.4 4.9 copy.128
  341.3 5.9 reshape.282
  347.3 1.1 copy-done.4
  348.4 1.3 copy.122
  350.2 0.7 reduce.3
  351.0 4.4 copy.121
  355.4 75.5 %all-to-all-done.2 = bf16[16,2,128,800]{2,3,1,0:T(8,128)(2,1)} async-done(((bf16[16,2,128,800]{2,3,1,0:T(8,128)(2,1)}), bf16[16,2,128,800]{2,3,1,0:T(8,128)(2,1)}, u32[]{:S(2)}, u32[]{:S(2)}) %all-to-all-start.2) | async-done | bytes 6553632 | tf_op jit(solution)/shard_map/all_to_all | solution.py:153
  431.0 11.0 %copy.127 = bf16[16,2,128,800]{3,2,1,0:T(8,128)(2,1)} copy(bf16[16,2,128,800]{2,3,1,0:T(8,128)(2,1)} %all-to-all-done.2) | data formatting | bytes 13107200 | tf_op jit(solution)/shard_map/all_to_all | solution.py:153
  442.0 13.6 %reshape.281 = bf16[32,102400]{1,0:T(8,128)(2,1)} reshape(bf16[16,2,128,800]{3,2,1,0:T(8,128)(2,1)} %copy.127) | data formatting | bytes 13107200 | tf_op jit(solution)/shard_map/reshape | solution.py:161
  455.6 5.1 fusion.20
  460.8 6.6 multiply_add_fusion
  467.4 11.1 %scatter_custom_fusion = f32[512,800]{1,0:T(8,128)S(1)} fusion(s32[1024]{0:T(1024)S(1)} %bitcast.114, f32[1024,400]{1,0:T(8,128)} %get-tuple-element.249, f32[]{:T(128)} %constant.164, f32[1024,400]{1,0:T(8,128)} %get-tuple-element.248, f32[]{:T(128)} %constant.133.clone.1), kind=kCustom, calls=%fused_computation.32 | custom fusion | flops 1638400 | bytes 4915208 | tf_op jit(solution)/shard_map/scatter-add | solution.py:132
  479.3 1.3 subtract_convert_fusion.2
  480.6 2.1 copy.129
  482.8 171.9 %all-reduce.8.cloned.1.call-done = f32[8,102400]{1,0:T(8,128)} async-done(((f32[8,102400]{1,0:T(8,128)}), f32[8,102400]{1,0:T(8,128)}) %all-reduce.8.cloned.1.call-update) | async-done | bytes 3276816 | tf_op jit(solution)/shard_map/psum | solution.py:168
  654.7 116.7 %all-reduce.6.cloned.1.call-done = f32[4,102400]{1,0:T(4,128)} async-done(((f32[4,102400]{1,0:T(4,128)}), f32[4,102400]{1,0:T(4,128)}) %all-reduce.6.cloned.1.call-update) | async-done | bytes 1638416 | tf_op jit(solution)/shard_map/psum | solution.py:37
  771.4 5.1 broadcast_multiply_fusion
  776.5 3.0 mul.159
  779.7 3.1 mul.157
  783.4 1.3 subtract_convert_fusion.1
  784.7 2.2 copy.130
  (95 shorter events, 6.2 us)
Async XLA Ops:
  15.6 7.8 copy-start.15
  15.6 7.9 copy-start.3
  15.6 211.3 %all-to-all-start = ((bf16[16,4,128,800]{2,3,1,0:T(8,128)(2,1)}), bf16[16,4,128,800]{2,3,1,0:T(8,128)(2,1)}, u32[]{:S(2)}, u32[]{:S(2)}) async-start(bf16[16,4,128,800]{2,3,1,0:T(8,128)(2,1)} %stack.2), calls=%async_computation | async-start | bytes 26214400 | tf_op jit(solution)/shard_map/all_to_all | solution.py:70
  23.3 253.8 %all-reduce.4.cloned.1.call-start = ((), (), s32[]{:S(2)}) async-start(), calls=%async_computation.3 | async-start | bytes 3670016 | tf_op jit(solution)/shard_map/psum | solution.py:80
  25.7 3.8 copy-start.9
  29.5 0.7 copy-start.12
  30.2 3.1 copy-start.10
  46.4 1.8 copy-start.1
  48.3 2.4 copy-start.11
  48.3 3.1 copy-start.17
  48.3 3.3 copy-start.16
  49.5 3.4 copy-start.6
  226.9 104.6 %all-to-all-start.1 = ((s32[16,1,2]{2,1,0:T(1,128)}), s32[16,1,2]{2,1,0:T(1,128)S(1)}, u32[]{:S(2)}, u32[]{:S(2)}) async-start(s32[16,1,2]{2,1,0:T(1,128)} %bitcast.14), calls=%async_computation.1 | async-start | bytes 16384 | tf_op jit(solution)/shard_map/all_to_all | solution.py:154
  277.1 3.1 copy-start.2
  277.1 3.9 copy-start.18
  280.2 4.1 copy-start
  280.2 2.7 copy-start.7
  284.3 1.7 copy-start.8
  291.9 3.1 copy-start.2
  291.9 3.9 copy-start.18
  294.9 4.1 copy-start
  295.0 2.7 copy-start.7
  299.1 1.7 copy-start.8
  331.6 99.4 %all-to-all-start.2 = ((bf16[16,2,128,800]{2,3,1,0:T(8,128)(2,1)}), bf16[16,2,128,800]{2,3,1,0:T(8,128)(2,1)}, u32[]{:S(2)}, u32[]{:S(2)}) async-start(bf16[16,2,128,800]{2,3,1,0:T(8,128)(2,1)} %bitcast.87), calls=%async_computation.2 | async-start | bytes 13107200 | tf_op jit(solution)/shard_map/all_to_all | solution.py:153
  336.2 318.5 %all-reduce.8.cloned.1.call-start = ((), (), s32[]{:S(2)}) async-start(), calls=%async_computation.5 | async-start | bytes 6553600 | tf_op jit(solution)/shard_map/psum | solution.py:168
  347.2 1.1 copy-start.4
  347.3 424.1 %all-reduce.6.cloned.1.call-start = ((), (), s32[]{:S(2)}) async-start(), calls=%async_computation.4 | async-start | bytes 3276800 | tf_op jit(solution)/shard_map/psum | solution.py:37
  467.4 11.3 %copy-start.13 = (f32[512]{0:T(512)S(1)}, f32[512]{0:T(512)}, u32[]{:S(2)}) copy-start(f32[512]{0:T(512)} %param.17) | copy-start | bytes 6148
  779.7 3.1 copy-start.14
  779.7 3.7 copy-start.5
Sparse Core Ops, SparseCore 0:
  29.6 247.4 all-reduce.3
  347.4 307.2 all-reduce.7
  657.1 114.2 all-reduce.5
